TPU v7x, 128 devices: a whole 4x4x4 slice. The times are simulated.
128 devices in a mesh: sky: 32 (over y, z, core), band: 4 (over x).
Axes of the slice: x: 4, y: 4, z: 4, core: 2. Of those that a mesh axis runs over, the one named last changes fastest.
Arguments:
- exposures: bfloat16 [32, 4, 1024, 1024], P('sky', 'band'), may hold values from -6 to 6
- inv_variance: bfloat16 [32, 4, 1024, 1024], P('sky', 'band'), may hold values from 0.25 to 4
- mask_planes: int32 [32, 4, 2, 35], P('sky', 'band'), may hold values from 0 to 1073741823, as said below
- sky_columns: int32 [32, 4, 8], replicated, may hold values from 0 to 31, as said below
- basis_rows: float32 [9, 25], replicated, may hold values from -1 to 1
- basis_cols: float32 [9, 25], replicated, may hold values from -1 to 1
- match_coeffs: float32 [32, 4, 9], P('sky', 'band'), may hold values from -2 to 2
- detect_taps: float32 [4, 31], P('band'), may hold values from 0.05 to 0.3
Outputs:
- difference: bfloat16 [32, 4, 1024, 1024], P('sky', 'band')
- detection: float32 [1024, 4096], P('band', 'sky')
Inputs may be any that keep to these rules, and one draw needn't show every extreme that they name: Each row sky_columns[e, b] holds 8 consecutive sky tile columns in order, counted modulo 32; every sky tile column is covered by some exposure of every band. Bit j of mask_planes[e, b, 0, w] marks pixel column 30 w + j of that exposure as bad and bit j of mask_planes[e, b, 1, w] pixel row 30 w + j; bits past 1024 are ignored. In every draw some word has all 30 bits set.
All inputs are finite; a program needn't handle non-finite values.
Results may differ from a plain program's by a relative error of at most 0.0095.
Values may be sent and summed in bfloat16 or wider, within the bound.
A program may use at most 128 MiB of HBM per device.

v0:
```python
import jax
import jax.numpy as jnp
from jax import lax
from jax.sharding import PartitionSpec as P

TILE = 128
NB = 9
TAPS = 25
DTAPS = 31


def with_halo(block, sides, width):
    for axis, dim in sides:
        count = lax.axis_size(axis)
        forward = [(i, i + 1) for i in range(count - 1)]
        forward.append((count - 1, 0))
        backward = [(target, source) for source, target in forward]
        low = lax.ppermute(
            lax.slice_in_dim(block, block.shape[dim] - width, None, axis=dim), axis, forward
        )
        high = lax.ppermute(lax.slice_in_dim(block, 0, width, axis=dim), axis, backward)
        block = jnp.concatenate([low, block, high], axis=dim)
    return block


def cut_along(value, dim, length):
    dims = value.shape
    pieces = value.reshape(*dims[:dim], length, dims[dim] // length, *dims[dim + 1 :])
    return jnp.moveaxis(pieces, dim, 0)


def sum_at_owner(value, axis, dim):
    pieces = cut_along(value, dim, lax.axis_size(axis))
    arrived = lax.all_to_all(pieces, axis, split_axis=0, concat_axis=0, tiled=True)
    return arrived.sum(axis=0)


def band_matrix(tap_rows, window_width):
    offsets = (
        jnp.arange(window_width, dtype=jnp.int32)[:, None]
        - jnp.arange(TILE, dtype=jnp.int32)[None, :]
    )
    selector = (
        offsets[:, :, None] == jnp.arange(tap_rows.shape[1], dtype=jnp.int32)[None, None, :]
    ).astype(jnp.float32)
    return jnp.einsum(
        "wtl,kl->kwt", selector, tap_rows.astype(jnp.float32), precision=lax.Precision.HIGHEST
    ).astype(jnp.bfloat16)


def keep_pixels(planes, side_length):
    places = jnp.arange(side_length, dtype=jnp.int32)
    column_bits = jnp.bitwise_and(jnp.right_shift(planes[0][places // 30], places % 30), 1)
    row_bits = jnp.bitwise_and(jnp.right_shift(planes[1][places // 30], places % 30), 1)
    return jnp.logical_and(row_bits[:, None] == 0, column_bits[None, :] == 0)


def psf_match(picture, column_taps, row_taps):
    side_length = picture.shape[1]
    block_count = side_length // TILE
    margin = TAPS // 2
    width_full = TILE + 2 * margin
    padded = jnp.pad(picture, ((0, 0), (margin, margin)))
    blocks = jnp.stack(
        [
            padded[:, TILE * block_index : TILE * block_index + width_full]
            for block_index in range(block_count)
        ],
        0,
    )
    column_band = band_matrix(column_taps, width_full)
    column_pass = jnp.einsum(
        "jyw,kwt->kyjt", blocks, column_band, preferred_element_type=jnp.float32
    )
    column_pass = column_pass.reshape(NB, side_length, side_length).astype(jnp.bfloat16)
    row_padded = jnp.pad(column_pass, ((0, 0), (margin, margin), (0, 0)))
    row_blocks = jnp.stack(
        [
            row_padded[:, TILE * block_index : TILE * block_index + width_full, :]
            for block_index in range(block_count)
        ],
        0,
    )
    row_band = band_matrix(row_taps, width_full)
    summed = jnp.einsum("ikwx,kwt->itx", row_blocks, row_band, preferred_element_type=jnp.float32)
    return summed.reshape(side_length, side_length).astype(jnp.bfloat16)


def average_pieces(pieces):
    matched_in, weight_in = pieces
    weight_float = weight_in.astype(jnp.float32)
    numer = jnp.sum(weight_float * matched_in.astype(jnp.float32), axis=1)
    denom = jnp.sum(weight_float, axis=1)
    return (numer / jnp.maximum(denom, 1.0)).astype(jnp.bfloat16)


def subtract_template(template, matched, own_columns, side_length, sky_count):
    gathered = lax.all_gather(template, "sky", axis=1, tiled=True).reshape(
        side_length, sky_count, TILE
    )
    picked = jnp.take(gathered, own_columns, axis=1).reshape(side_length, side_length)
    return (matched.astype(jnp.float32) - picked.astype(jnp.float32)).astype(jnp.bfloat16)


def body(
    exposures,
    inv_variance,
    mask_planes,
    sky_columns,
    basis_rows,
    basis_cols,
    match_coeffs,
    detect_taps,
):
    picture = exposures[0, 0]
    side_length = picture.shape[0]
    block_count = side_length // TILE
    sky_count = lax.axis_size("sky")
    own_sky = lax.axis_index("sky")
    own_band = lax.axis_index("band")
    column_taps = (match_coeffs[0, 0][:, None] * basis_cols).astype(jnp.bfloat16)
    matched = psf_match(picture, column_taps, basis_rows.astype(jnp.bfloat16))
    keep = keep_pixels(mask_planes[0, 0], side_length)
    variance_inv = inv_variance[0, 0]
    weight = jnp.where(keep, variance_inv, jnp.zeros_like(variance_inv))
    own_columns = sky_columns[own_sky, own_band]
    empty_slots = jnp.zeros((side_length, sky_count, TILE), jnp.bfloat16)
    send_matched = empty_slots.at[:, own_columns, :].set(
        matched.reshape(side_length, block_count, TILE)
    )
    send_weight = empty_slots.at[:, own_columns, :].set(
        weight.reshape(side_length, block_count, TILE)
    )
    template = average_pieces(
        (
            lax.all_to_all(send_matched, "sky", split_axis=1, concat_axis=1, tiled=True),
            lax.all_to_all(send_weight, "sky", split_axis=1, concat_axis=1, tiled=True),
        )
    )
    difference = subtract_template(template, matched, own_columns, side_length, sky_count)
    margin = DTAPS // 2
    width_full = TILE + 2 * margin
    filter_band = band_matrix(detect_taps.astype(jnp.bfloat16), width_full)[0]
    widened = with_halo(template, (("sky", 1),), margin)
    smoothed = jnp.dot(widened, filter_band, preferred_element_type=jnp.float32).astype(
        jnp.bfloat16
    )
    smooth_padded = jnp.pad(smoothed, ((margin, margin), (0, 0)))
    smooth_blocks = jnp.stack(
        [
            smooth_padded[TILE * block_index : TILE * block_index + width_full]
            for block_index in range(block_count)
        ],
        0,
    )
    filtered = jnp.einsum(
        "iwx,wt->itx", smooth_blocks, filter_band, preferred_element_type=jnp.float32
    ).reshape(side_length, TILE)
    power = filtered * filtered
    detection = sum_at_owner(power, "band", 0)
    return (difference[None, None], detection)


def solution(mesh):
    in_specs = (
        P("sky", "band", None, None),
        P("sky", "band", None, None),
        P("sky", "band", None, None),
        P(),
        P(),
        P(),
        P("sky", "band", None),
        P("band", None),
    )
    out_specs = (P("sky", "band", None, None), P("band", "sky"))
    return jax.shard_map(body, mesh=mesh, in_specs=in_specs, out_specs=out_specs, check_vma=False)
```

profile of v0, /device:TPU:1, one launch (start us, length us, event | category | flops | bytes accessed | tf_op | source)
XLA Modules:
  0.0 444.7 jit_solution(8928743750772134446)
XLA Ops:
  7.2 2.9 copy.63
  10.2 0.1 fusion.40
  10.2 0.1 fusion.39
  10.3 0.1 fusion.38
  10.4 0.1 fusion.37
  10.5 0.1 fusion.36
  10.6 0.1 fusion.35
  10.8 0.3 copy-done.5
  11.0 0.6 fusion.19
  11.6 9.2 %convolution_convert_fusion = bf16[9,128,8,1024]{3,1,2,0:T(8,128)(2,1)} fusion(bf16[8,1024,152]{1,2,0:T(8,128)(2,1)S(1)} %fusion.34, bf16[9,152,128,1]{2,0,1,3:T(8,128)(2,1)S(1)} %fusion.19), kind=kOutput, calls=%fused_computation.8 | convolution fusion | flops 2878341120 | bytes 21714944 | tf_op jit(solution)/shard_map/jyw,kwt->kyjt/dot_general | solution.py:72
  20.8 24.6 %copy.65 = bf16[9,1024,1024]{2,1,0:T(8,128)(2,1)} copy(bf16[9,1024,1024]{1,2,0:T(8,128)(2,1)} %bitcast.238) | data formatting | bytes 37748736 | tf_op jit(solution)/shard_map/convert_element_type | solution.py:75
  45.4 4.3 fusion.2
  49.8 3.8 copy-done.2
  53.6 2.5 fusion.10
  56.1 2.4 fusion.9
  58.5 2.5 fusion.8
  61.0 2.5 fusion.7
  63.5 2.4 fusion.6
  65.9 2.4 fusion.5
  68.4 2.4 fusion.4
  70.8 0.6 fusion.20
  71.4 9.9 %bitcast_convert_fusion = bf16[128,8,1024]{2,0,1:T(8,128)(2,1)S(1)} fusion(bf16[8,9,152,1024]{3,2,1,0:T(8,128)(2,1)} %fusion.4, bf16[9,152,128]{2,0,1:T(8,128)(2,1)S(1)} %fusion.20), kind=kOutput, calls=%fused_computation.9 | convolution fusion | flops 2869952512 | bytes 24860672 | tf_op jit(solution)/shard_map/ikwx,kwt->itx/dot_general | solution.py:85
  81.3 0.6 copy.87
  81.9 1.7 copy.103
  83.6 0.2 dynamic-slice_reduce_fusion
  83.8 5.1 %broadcast_in_dim.18.clone.1 = bf16[1024,32,128]{2,0,1:T(8,128)(2,1)} broadcast(bf16[]{:T(256)} %constant.31.clone.1), dimensions={} | broadcast | bytes 8388610 | tf_op jit(solution)/shard_map/broadcast_in_dim | solution.py:127
  88.9 5.7 %scatter_fusion.1 = bf16[1024,32,128]{2,0,1:T(8,128)(2,1)} fusion(bf16[1024,32,128]{2,0,1:T(8,128)(2,1)} %broadcast_in_dim.18.clone.1, s32[8]{0:T(128)S(1)} %fusion.61, bf16[8,1024,128]{2,1,0:T(8,128)(2,1)} %bitcast.250), kind=kCustom, calls=%fused_computation.2 | custom fusion | bytes 6291488 | tf_op jit(solution)/shard_map/scatter | solution.py:128
  94.6 9.6 %all-to-all-start.1 = ((bf16[1024,32,128]{2,0,1:T(8,128)(2,1)}), bf16[1024,32,128]{2,0,1:T(8,128)(2,1)}, u32[]{:S(2)}, u32[]{:S(2)}) async-start(bf16[1024,32,128]{2,0,1:T(8,128)(2,1)} %scatter_fusion.1), calls=%async_computation.1 | async-start | bytes 16777216 | tf_op jit(solution)/shard_map/all_to_all | solution.py:136
  104.3 2.2 copy.86
  107.7 0.7 fusion.67
  108.4 0.7 fusion.64
  109.1 4.5 %compare_select_fusion.2 = s32[1024,1]{0,1:T(1,128)S(1)} fusion(s32[]{:T(128)} %bitcast.97, s32[]{:T(128)} %bitcast.98, s32[]{:T(128)} %bitcast.99, s32[]{:T(128)} %bitcast.100, s32[]{:T(128)} %bitcast.101, s32[]{:T(128)} %bitcast.103, s32[]{:T(128)} %bitcast.102), kind=kLoop, calls=%fused_computation.125 | loop fusion | flops 23552 | bytes 4124 | tf_op jit(solution)/shard_map/gather | solution.py:53
  113.6 0.7 fusion.65
  114.3 0.7 fusion.66
  115.0 4.4 compare_select_fusion.1
  119.5 17.3 %fusion.49 = pred[8,128]{1,0:T(8,128)(4,1)S(1)} fusion(pred[1024]{0:T(1024)(128)(4,1)S(1)} %compare_reduce_fusion, pred[1024]{0:T(1024)(128)(4,1)S(1)} %compare_reduce_fusion.1, pred[1024]{0:T(1024)(128)(4,1)S(1)} %compare_reduce_fusion.2, pred[1024]{0:T(1024)(128)(4,1)S(1)} %compare_reduce_fusion.3, pred[1024]{0:T(1024)(128)(4,1)S(1)} %compare_reduce_fusion.4, ...), kind=kLoop, calls=%fused_computation.147 | loop fusion | flops 39936 | bytes 33904 | tf_op jit(solution)/shard_map/eq | solution.py:55
  136.8 17.6 %fusion.46 = pred[1024]{0:T(1024)(128)(4,1)S(1)} fusion(pred[1024]{0:T(1024)(128)(4,1)S(1)} %compare_reduce_fusion, pred[1024]{0:T(1024)(128)(4,1)S(1)} %compare_reduce_fusion.1, pred[1024]{0:T(1024)(128)(4,1)S(1)} %compare_reduce_fusion.2, pred[1024]{0:T(1024)(128)(4,1)S(1)} %compare_reduce_fusion.3, pred[1024]{0:T(1024)(128)(4,1)S(1)} %compare_reduce_fusion.4, ...), kind=kLoop, calls=%fused_computation.144 | loop fusion | flops 37888 | bytes 33904 | tf_op jit(solution)/shard_map/eq | solution.py:55
  154.4 2.1 fusion.16
  156.4 5.1 %broadcast_in_dim.18.clone = bf16[1024,32,128]{2,0,1:T(8,128)(2,1)} broadcast(bf16[]{:T(256)} %constant.31.clone.1), dimensions={} | broadcast | bytes 8388610 | tf_op jit(solution)/shard_map/broadcast_in_dim | solution.py:127
  161.5 5.8 %scatter_fusion = bf16[1024,32,128]{2,0,1:T(8,128)(2,1)} fusion(bf16[1024,32,128]{2,0,1:T(8,128)(2,1)} %broadcast_in_dim.18.clone, s32[8]{0:T(128)S(1)} %fusion.61, bf16[8,1024,128]{2,1,0:T(8,128)(2,1)} %fusion.16), kind=kCustom, calls=%fused_computation.1 | custom fusion | bytes 6291488 | tf_op jit(solution)/shard_map/scatter | solution.py:131
  167.3 45.5 %all-to-all-done.1 = bf16[1024,32,128]{2,0,1:T(8,128)(2,1)} async-done(((bf16[1024,32,128]{2,0,1:T(8,128)(2,1)}), bf16[1024,32,128]{2,0,1:T(8,128)(2,1)}, u32[]{:S(2)}, u32[]{:S(2)}) %all-to-all-start.1) | async-done | bytes 8388640 | tf_op jit(solution)/shard_map/all_to_all | solution.py:136
  212.8 117.1 %all_to_all.15 = bf16[1024,32,128]{2,0,1:T(8,128)(2,1)} all-to-all(bf16[1024,32,128]{2,0,1:T(8,128)(2,1)} %scatter_fusion), channel_id=1, replica_groups=mesh['sky'=32,'band'=4] {'sky'}, dimensions={1} | all-to-all | bytes 16777216 | tf_op jit(solution)/shard_map/all_to_all | solution.py:137
  329.9 9.0 %convert_reduce_fusion = (f32[1024,128]{1,0:T(8,128)S(1)}, f32[1024,128]{1,0:T(8,128)S(1)}) fusion(bf16[1024,32,128]{2,0,1:T(8,128)(2,1)} %all_to_all.15, bf16[1024,32,128]{2,0,1:T(8,128)(2,1)} %all-to-all-done.1), kind=kLoop, calls=%fused_computation.3 | loop fusion | flops 20709376 | bytes 17825792 | tf_op jit(solution)/shard_map/reduce_sum | solution.py:93
  338.9 0.8 divide_convert_fusion
  339.8 0.3 iota_compare_fusion
  340.1 0.5 fusion.11
  340.7 0.1 fusion.63
  340.8 0.3 collective-permute-start
  341.1 0.2 collective-permute-start.1
  341.4 3.0 copy.78
  344.5 2.8 collective-permute-done.1
  347.2 1.4 convolution_convert_fusion.1
  348.8 1.0 convolution_multiply_fusion
  349.9 4.0 all-to-all-start.2
  353.9 0.1 broadcast_bitcast_fusion
  354.0 6.8 %all-to-all-done.2 = f32[4,256,128]{2,1,0:T(8,128)S(1)} async-done(((f32[4,256,128]{2,1,0:T(8,128)}), f32[4,256,128]{2,1,0:T(8,128)S(1)}, u32[]{:S(2)}, u32[]{:S(2)}) %all-to-all-start.2) | async-done | bytes 524320 | tf_op jit(solution)/shard_map/all_to_all | solution.py:34
  360.8 0.7 reduce_sum.29
  361.5 36.1 %all-gather.2.cloned.1.call-done = bf16[1024,4096]{1,0:T(8,128)(2,1)} async-done(((bf16[1024,128]{1,0:T(8,128)(2,1)}), bf16[1024,4096]{1,0:T(8,128)(2,1)}) %all-gather.2.cloned.1.call-update) | async-done | bytes 8388624 | tf_op jit(solution)/shard_map/all_gather | solution.py:98
  397.6 11.9 %copy.75 = bf16[1024,4096]{0,1:T(8,128)(2,1)} copy(bf16[1024,4096]{1,0:T(8,128)(2,1)} %all-gather.2.cloned.1.call-done) | data formatting | bytes 16777216 | tf_op jit(solution)/shard_map/all_gather | solution.py:98
  409.5 11.9 %copy.76 = bf16[1024,32,128]{2,0,1:T(8,128)(2,1)} copy(bf16[1024,32,128]{0,2,1:T(8,128)(2,1)} %bitcast.239) | data formatting | bytes 16777216 | tf_op jit(solution)/shard_map/reshape | solution.py:98
  421.4 5.5 %gather_fusion = bf16[8,1024,128]{2,1,0:T(8,128)(2,1)} fusion(bf16[1024,32,128]{2,0,1:T(8,128)(2,1)} %copy.76, s32[1024]{0:T(1024)S(1)} %pad_clamp_fusion), kind=kCustom, calls=%fused_computation | custom fusion | bytes 4194336 | tf_op jit(solution)/shard_map/jit(_take)/gather | solution.py:101
  426.9 2.9 copy.77
  429.8 4.1 subtract_convert_fusion
  433.9 3.9 copy.79
  (62 shorter events, 1.7 us)
Async XLA Ops:
  7.2 76.4 %copy-start = (s32[32,4,8]{0,2,1:T(8,128)S(1)}, s32[32,4,8]{0,2,1:T(8,128)}, u32[]{:S(2)}) copy-start(s32[32,4,8]{0,2,1:T(8,128)} %param.11) | copy-start | bytes 12292
  10.3 0.7 copy-start.5
  10.3 0.7 copy-start.6
  45.4 8.2 %copy-start.2 = (bf16[9,1024,1024]{2,1,0:T(8,128)(2,1)S(1)}, bf16[9,1024,1024]{2,1,0:T(8,128)(2,1)}, u32[]{:S(2)}) copy-start(bf16[9,1024,1024]{2,1,0:T(8,128)(2,1)} %copy.65) | copy-start | bytes 56623108
  68.4 2.4 copy-start.7
  94.6 118.2 %all-to-all-start.1 = ((bf16[1024,32,128]{2,0,1:T(8,128)(2,1)}), bf16[1024,32,128]{2,0,1:T(8,128)(2,1)}, u32[]{:S(2)}, u32[]{:S(2)}) async-start(bf16[1024,32,128]{2,0,1:T(8,128)(2,1)} %scatter_fusion.1), calls=%async_computation.1 | async-start | bytes 16777216 | tf_op jit(solution)/shard_map/all_to_all | solution.py:136
  104.2 3.4 copy-start.4
  104.3 293.3 %all-gather.2.cloned.1.call-start = ((), (), s32[]{:S(2)}) async-start(), calls=%async_computation.3 | async-start | bytes 8650752 | tf_op jit(solution)/shard_map/all_gather | solution.py:98
  329.9 10.2 %copy-start.8 = (f32[1,31]{1,0:T(1,128)S(1)}, f32[1,31]{1,0:T(1,128)}, u32[]{:S(2)}) copy-start(f32[1,31]{1,0:T(1,128)} %param.15) | copy-start | bytes 376
  339.7 0.9 copy-start.3
  340.8 3.7 collective-permute-start
  341.1 6.1 %collective-permute-start.1 = (bf16[1024,15]{1,0:T(8,128)(2,1)S(1)}, bf16[1024,15]{1,0:T(8,128)(2,1)}, u32[]{:S(2)}, u32[]{:S(2)}) collective-permute-start(bf16[1024,15]{1,0:T(8,128)(2,1)S(1)} %get-tuple-element.11), channel_id=1, source_target_pairs={{4,0},{8,4},{12,8},{16,12},{20,16},{24,20},{28,24},{32,28},{36,32}... | collective-permute-start | bytes 92168 | tf_op jit(solution)/shard_map/ppermute | solution.py:21
  349.9 11.0 %all-to-all-start.2 = ((f32[4,256,128]{2,1,0:T(8,128)}), f32[4,256,128]{2,1,0:T(8,128)S(1)}, u32[]{:S(2)}, u32[]{:S(2)}) async-start(f32[4,256,128]{2,1,0:T(8,128)} %bitcast.124), calls=%async_computation.2 | async-start | bytes 1048576 | tf_op jit(solution)/shard_map/all_to_all | solution.py:34
  429.8 8.1 %copy-start.1 = (s32[32,4,8]{0,2,1:T(8,128)S(1)}, s32[32,4,8]{0,2,1:T(8,128)}, u32[]{:S(2)}) copy-start(s32[32,4,8]{0,2,1:T(8,128)} %param.11) | copy-start | bytes 12292
Sparse Core Ops, SparseCore 0:
  339.9 57.6 all-gather.1
where the time goes:
time: 447 us; the launch traced here: 445 us
  local copies, waits for them, and re-layouts  123 us (28%)
  blocking collectives  117 us (26%)
  waiting for transfers between devices  91.2 us (20%)
  other arithmetic  61.9 us (14%)
  matrix products  23.2 us (5%)
  starting transfers between devices  14.3 us (3%)
  between operations  14.3 us (3%)
    all_to_all x1, blocking collectives, body(): lax.all_to_all(send_weight, 'sky', split_axis=1, concat_axis=1, tiled=True)  117 us
    all_to_all x1, waiting for transfers between devices, body(): lax.all_to_all(send_matched, 'sky', split_axis=1, concat_axis=1, tiled=True)  45.5 us
    all_gather x1, waiting for transfers between devices, subtract_template(): lax.all_gather(template, 'sky', axis=1, tiled=True)  36.1 us
    eq x2, other arithmetic, keep_pixels(): return jnp.logical_and(row_bits[:, None] == 0, column_bits[None, :] == 0)  34.9 us
    unnamed x43, local copies, waits for them, and re-layouts  33.6 us
    convert_element_type x1, local copies, waits for them, and re-layouts, psf_match(): column_pass.reshape(NB, side_length, side_length).astype(jnp.bfloat16)  24.6 us
    all_gather x1, local copies, waits for them, and re-layouts, subtract_template(): lax.all_gather(template, 'sky', axis=1, tiled=True)  11.9 us
    reshape x1, local copies, waits for them, and re-layouts, subtract_template(): lax.all_gather(template, 'sky', axis=1, tiled=True)  11.9 us
  transfers between devices with their start and end apart: 5, of which 5 were waited for; matrix products, arithmetic and copies ran while one was open for 16% of the time, Pallas kernels for 0%

commit v1 on v0

--- a/solution.py
+++ b/solution.py
@@ -1,3 +1,4 @@
+import functools
 import jax
 import jax.numpy as jnp
 from jax import lax
@@ -7,6 +8,18 @@
 NB = 9
 TAPS = 25
 DTAPS = 31
+
+
+def _balance_cards(vals, axis_no, array_axis):
+    return jnp.concatenate(
+        jax.lax.all_to_all(
+            jnp.stack(jnp.split(vals, jax.lax.axis_size("sky"), axis=axis_no)), "sky", 0, 0
+        ),
+        axis=array_axis,
+    )
+
+
+hubs_refer = functools.partial(_balance_cards, axis_no=1, array_axis=1)
 
 
 def with_halo(block, sides, width):
@@ -134,7 +147,7 @@
     template = average_pieces(
         (
             lax.all_to_all(send_matched, "sky", split_axis=1, concat_axis=1, tiled=True),
-            lax.all_to_all(send_weight, "sky", split_axis=1, concat_axis=1, tiled=True),
+            hubs_refer(send_weight),
         )
     )
     difference = subtract_template(template, matched, own_columns, side_length, sky_count)

time: 447 us -> 511 us (1.14)
  blocking collectives: 117 us -> 0 us
  waiting for transfers between devices: 91.2 us -> 170 us
  local copies, waits for them, and re-layouts: 123 us -> 181 us
  starting transfers between devices: 14.3 us -> 53.9 us
    all_to_all x1 -> x0, blocking collectives: 117 us -> none  [body(): lax.all_to_all(send_weight, 'sky', split_axis=1, concat_axis=1, tiled=True)]
    all_to_all x1, waiting for transfers between devices: 45.5 us -> 104 us  [body(): lax.all_to_all(send_matched, 'sky', split_axis=1, concat_axis=1, tiled=True)]
    unnamed x43 -> x72, local copies, waits for them, and re-layouts: 33.6 us -> 85 us
    all_to_all x0 -> x1, waiting for transfers between devices: none -> 20.4 us  [_balance_cards(): jax.lax.all_to_all(jnp.stack(jnp.split(vals, jax.lax.axis_size('sky'), ax...]
    all_to_all x1, starting transfers between devices: 9.63 us -> 22.7 us  [body(): lax.all_to_all(send_matched, 'sky', split_axis=1, concat_axis=1, tiled=True)]
    ppermute x1, starting transfers between devices: 0.34 us -> 12 us  [with_halo(): lax.ppermute(lax.slice_in_dim(block, block.shape[dim] - width, None, axis...]
    all_to_all x0 -> x1, starting transfers between devices: none -> 9.62 us  [_balance_cards(): jax.lax.all_to_all(jnp.stack(jnp.split(vals, jax.lax.axis_size('sky'), ax...]
    reduce_sum x0 -> x1, other arithmetic: none -> 8.45 us  [average_pieces(): numer = jnp.sum(weight_float * matched_in.astype(jnp.float32), axis=1)]
  transfers between devices with their start and end apart: 5 -> 6, of which waited for: 5 -> 5; matrix products, arithmetic and copies ran while one was open for 16% -> 19% of each run, Pallas kernels for 0% -> 0%
where the time goes in v1:
time: 511 us; the launch traced here: 507 us
  local copies, waits for them, and re-layouts  181 us (35%)
  waiting for transfers between devices  170 us (33%)
  other arithmetic  64.7 us (13%)
  starting transfers between devices  53.9 us (11%)
  matrix products  22.3 us (4%)
  between operations  14.4 us (3%)
    all_to_all x1, waiting for transfers between devices, body(): lax.all_to_all(send_matched, 'sky', split_axis=1, concat_axis=1, tiled=True)  104 us
    unnamed x72, local copies, waits for them, and re-layouts  85 us
    all_gather x1, waiting for transfers between devices, subtract_template(): lax.all_gather(template, 'sky', axis=1, tiled=True)  38.4 us
    eq x2, other arithmetic, keep_pixels(): return jnp.logical_and(row_bits[:, None] == 0, column_bits[None, :] == 0)  34.9 us
    convert_element_type x1, local copies, waits for them, and re-layouts, psf_match(): column_pass.reshape(NB, side_length, side_length).astype(jnp.bfloat16)  24.6 us
    all_to_all x1, starting transfers between devices, body(): lax.all_to_all(send_matched, 'sky', split_axis=1, concat_axis=1, tiled=True)  22.7 us
    all_to_all x1, waiting for transfers between devices, _balance_cards(): jax.lax.all_to_all(jnp.stack(jnp.split(vals, jax.lax.axis_size('sky'), ax...  20.4 us
    ppermute x1, starting transfers between devices, with_halo(): lax.ppermute(lax.slice_in_dim(block, block.shape[dim] - width, None, axis...  12 us
  transfers between devices with their start and end apart: 6, of which 5 were waited for; matrix products, arithmetic and copies ran while one was open for 19% of the time, Pallas kernels for 0%

profile of v1, /device:TPU:1, one launch (start us, length us, event | category | flops | bytes accessed | tf_op | source)
XLA Modules:
  0.0 507.0 jit_solution(10853572131441409011)
XLA Ops:
  8.3 2.1 fusion.98
  10.4 1.9 fusion.101
  12.3 2.1 fusion.99
  14.4 2.1 fusion.100
  16.7 2.2 copy.86
  18.9 4.5 compare_select_fusion.2
  23.4 4.3 compare_select_fusion.1
  27.8 17.4 %fusion.83 = pred[8,128]{1,0:T(8,128)(4,1)S(1)} fusion(pred[1024]{0:T(1024)(128)(4,1)S(1)} %compare_reduce_fusion, pred[1024]{0:T(1024)(128)(4,1)S(1)} %compare_reduce_fusion.1, pred[1024]{0:T(1024)(128)(4,1)S(1)} %compare_reduce_fusion.2, pred[1024]{0:T(1024)(128)(4,1)S(1)} %compare_reduce_fusion.3, pred[1024]{0:T(1024)(128)(4,1)S(1)} %compare_reduce_fusion.4, ...), kind=kLoop, calls=%fused_computation.213 | loop fusion | flops 39936 | bytes 33904 | tf_op jit(solution)/shard_map/eq | solution.py:68
  45.2 17.5 %fusion.80 = pred[1024]{0:T(1024)(128)(4,1)S(1)} fusion(pred[1024]{0:T(1024)(128)(4,1)S(1)} %compare_reduce_fusion, pred[1024]{0:T(1024)(128)(4,1)S(1)} %compare_reduce_fusion.1, pred[1024]{0:T(1024)(128)(4,1)S(1)} %compare_reduce_fusion.2, pred[1024]{0:T(1024)(128)(4,1)S(1)} %compare_reduce_fusion.3, pred[1024]{0:T(1024)(128)(4,1)S(1)} %compare_reduce_fusion.4, ...), kind=kLoop, calls=%fused_computation.210 | loop fusion | flops 37888 | bytes 33904 | tf_op jit(solution)/shard_map/eq | solution.py:68
  63.4 5.1 %broadcast_in_dim.18.clone = bf16[1024,32,128]{2,0,1:T(8,128)(2,1)} broadcast(bf16[]{:T(256)} %constant.31.clone.1), dimensions={} | broadcast | bytes 8388610 | tf_op jit(solution)/shard_map/broadcast_in_dim | solution.py:140
  68.5 5.1 scatter_fusion
  73.6 1.7 fusion.74
  81.9 1.7 fusion.69
  83.6 1.7 fusion.68
  85.3 1.7 fusion.67
  86.9 1.7 fusion.66
  91.9 1.7 fusion.63
  93.6 1.7 fusion.62
  98.6 1.7 fusion.59
  100.3 1.7 fusion.58
  102.0 1.7 fusion.57
  103.6 1.7 fusion.56
  105.3 1.7 fusion.55
  108.6 1.7 fusion.53
  110.3 1.7 fusion.52
  112.0 1.7 fusion.51
  113.6 1.7 fusion.50
  118.6 1.7 fusion.47
  120.3 1.7 fusion.46
  123.6 1.7 fusion.44
  125.3 1.7 fusion.43
  127.0 9.6 %all-to-all-start = ((bf16[32,1024,1,128]{3,1,2,0:T(8,128)(2,1)}), bf16[32,1024,1,128]{3,1,2,0:T(8,128)(2,1)}, u32[]{:S(2)}, u32[]{:S(2)}) async-start(bf16[32,1024,1,128]{3,1,2,0:T(8,128)(2,1)} %fusion.43), calls=%async_computation | async-start | bytes 16777216 | tf_op jit(solution)/shard_map/all_to_all | solution.py:15
  136.6 2.9 copy.63
  140.8 9.2 %convolution_convert_fusion = bf16[9,128,8,1024]{3,1,2,0:T(8,128)(2,1)} fusion(bf16[8,1024,152]{1,2,0:T(8,128)(2,1)S(1)} %fusion.36, bf16[9,152,128,1]{2,0,1,3:T(8,128)(2,1)S(1)} %fusion.21), kind=kOutput, calls=%fused_computation.10 | convolution fusion | flops 2878341120 | bytes 21714944 | tf_op jit(solution)/shard_map/jyw,kwt->kyjt/dot_general | solution.py:85
  150.0 24.6 %copy.65 = bf16[9,1024,1024]{2,1,0:T(8,128)(2,1)} copy(bf16[9,1024,1024]{1,2,0:T(8,128)(2,1)} %bitcast.377) | data formatting | bytes 37748736 | tf_op jit(solution)/shard_map/convert_element_type | solution.py:88
  174.6 4.3 fusion.4
  179.0 3.8 copy-done.2
  182.8 2.5 fusion.12
  185.2 2.4 fusion.11
  187.7 2.5 fusion.10
  190.2 2.5 fusion.9
  192.7 2.4 fusion.8
  195.1 2.4 fusion.7
  197.5 2.4 fusion.6
  200.6 9.9 %bitcast_convert_fusion = bf16[128,8,1024]{2,0,1:T(8,128)(2,1)S(1)} fusion(bf16[8,9,152,1024]{3,2,1,0:T(8,128)(2,1)} %fusion.6, bf16[9,152,128]{2,0,1:T(8,128)(2,1)S(1)} %fusion.22), kind=kOutput, calls=%fused_computation.11 | convolution fusion | flops 2869952512 | bytes 24860672 | tf_op jit(solution)/shard_map/ikwx,kwt->itx/dot_general | solution.py:98
  212.8 5.1 %broadcast_in_dim.18.clone.1 = bf16[1024,32,128]{2,0,1:T(8,128)(2,1)} broadcast(bf16[]{:T(256)} %constant.31.clone.1), dimensions={} | broadcast | bytes 8388610 | tf_op jit(solution)/shard_map/broadcast_in_dim | solution.py:140
  217.9 5.7 %scatter_fusion.1 = bf16[1024,32,128]{2,0,1:T(8,128)(2,1)} fusion(bf16[1024,32,128]{2,0,1:T(8,128)(2,1)} %broadcast_in_dim.18.clone.1, s32[8]{0:T(128)S(1)} %fusion.95, bf16[8,1024,128]{2,1,0:T(8,128)(2,1)} %bitcast.389), kind=kCustom, calls=%fused_computation.2 | custom fusion | bytes 6291488 | tf_op jit(solution)/shard_map/scatter | solution.py:141
  223.6 20.4 %all-to-all-done = bf16[32,1024,1,128]{3,1,2,0:T(8,128)(2,1)} async-done(((bf16[32,1024,1,128]{3,1,2,0:T(8,128)(2,1)}), bf16[32,1024,1,128]{3,1,2,0:T(8,128)(2,1)}, u32[]{:S(2)}, u32[]{:S(2)}) %all-to-all-start) | async-done | bytes 8388640 | tf_op jit(solution)/shard_map/all_to_all | solution.py:15
  244.1 22.7 %all-to-all-start.1 = ((bf16[1024,32,128]{2,0,1:T(8,128)(2,1)}), bf16[1024,32,128]{2,0,1:T(8,128)(2,1)}, u32[]{:S(2)}, u32[]{:S(2)}) async-start(bf16[1024,32,128]{2,0,1:T(8,128)(2,1)} %scatter_fusion.1), calls=%async_computation.1 | async-start | bytes 16777216 | tf_op jit(solution)/shard_map/all_to_all | solution.py:149
  266.8 4.7 fusion
  271.5 103.7 %all-to-all-done.1 = bf16[1024,32,128]{2,0,1:T(8,128)(2,1)} async-done(((bf16[1024,32,128]{2,0,1:T(8,128)(2,1)}), bf16[1024,32,128]{2,0,1:T(8,128)(2,1)}, u32[]{:S(2)}, u32[]{:S(2)}) %all-to-all-start.1) | async-done | bytes 8388640 | tf_op jit(solution)/shard_map/all_to_all | solution.py:149
  375.3 8.4 %fusion.2 = f32[1024,128]{1,0:T(8,128)S(1)} fusion(bf16[32,1024,1,128]{3,1,2,0:T(8,128)(2,1)} %all-to-all-done, bf16[1024,32,128]{2,0,1:T(8,128)(2,1)} %all-to-all-done.1), kind=kLoop, calls=%fused_computation.9 | loop fusion | flops 16646144 | bytes 17301504 | tf_op jit(solution)/shard_map/reduce_sum | solution.py:105
  386.6 5.5 %collective-permute-start.1 = (bf16[1024,15]{1,0:T(8,128)(2,1)S(1)}, bf16[1024,15]{1,0:T(8,128)(2,1)S(1)}, u32[]{:S(2)}, u32[]{:S(2)}) collective-permute-start(bf16[1024,15]{1,0:T(8,128)(2,1)S(1)} %get-tuple-element.9), channel_id=1, source_target_pairs={{4,0},{8,4},{12,8},{16,12},{20,16},{24,20},{28,24},{32,28},{36,32}... | collective-permute-start | bytes 92168 | tf_op jit(solution)/shard_map/ppermute | solution.py:34
  392.2 12.0 %collective-permute-start = (bf16[1024,15]{1,0:T(8,128)(2,1)S(1)}, bf16[1024,15]{1,0:T(8,128)(2,1)S(1)}, u32[]{:S(2)}, u32[]{:S(2)}) collective-permute-start(bf16[1024,15]{1,0:T(8,128)(2,1)S(1)} %get-tuple-element.8), channel_id=1, source_target_pairs={{0,4},{4,8},{8,12},{12,16},{16,20},{20,24},{24,28},{28,32},{32,36}... | collective-permute-start | bytes 92168 | tf_op jit(solution)/shard_map/ppermute | solution.py:31
  404.2 3.0 copy.78
  409.8 4.1 all-to-all-start.2
  414.0 6.9 %all-to-all-done.2 = f32[4,256,128]{2,1,0:T(8,128)S(1)} async-done(((f32[4,256,128]{2,1,0:T(8,128)}), f32[4,256,128]{2,1,0:T(8,128)S(1)}, u32[]{:S(2)}, u32[]{:S(2)}) %all-to-all-start.2) | async-done | bytes 524320 | tf_op jit(solution)/shard_map/all_to_all | solution.py:47
  421.5 38.4 %all-gather.2.cloned.1.call-done = bf16[1024,4096]{1,0:T(8,128)(2,1)} async-done(((bf16[1024,128]{1,0:T(8,128)(2,1)}), bf16[1024,4096]{1,0:T(8,128)(2,1)}) %all-gather.2.cloned.1.call-update) | async-done | bytes 8388624 | tf_op jit(solution)/shard_map/all_gather | solution.py:111
  459.9 11.9 %copy.75 = bf16[1024,4096]{0,1:T(8,128)(2,1)} copy(bf16[1024,4096]{1,0:T(8,128)(2,1)} %all-gather.2.cloned.1.call-done) | data formatting | bytes 16777216 | tf_op jit(solution)/shard_map/all_gather | solution.py:111
  471.9 11.9 %copy.76 = bf16[1024,32,128]{2,0,1:T(8,128)(2,1)} copy(bf16[1024,32,128]{0,2,1:T(8,128)(2,1)} %bitcast.378) | data formatting | bytes 16777216 | tf_op jit(solution)/shard_map/reshape | solution.py:111
  483.8 5.5 %gather_fusion = bf16[8,1024,128]{2,1,0:T(8,128)(2,1)} fusion(bf16[1024,32,128]{2,0,1:T(8,128)(2,1)} %copy.76, s32[1024]{0:T(1024)S(1)} %pad_clamp_fusion), kind=kCustom, calls=%fused_computation | custom fusion | bytes 4194336 | tf_op jit(solution)/shard_map/jit(_take)/gather | solution.py:114
  489.3 2.9 copy.77
  492.2 4.1 subtract_convert_fusion
  496.3 3.9 copy.79
  (94 shorter events, 32.4 us)
Async XLA Ops:
  7.2 9.3 %copy-start = (s32[32,4,8]{0,2,1:T(8,128)S(1)}, s32[32,4,8]{0,2,1:T(8,128)}, u32[]{:S(2)}) copy-start(s32[32,4,8]{0,2,1:T(8,128)} %param.11) | copy-start | bytes 12292
  127.0 117.1 %all-to-all-start = ((bf16[32,1024,1,128]{3,1,2,0:T(8,128)(2,1)}), bf16[32,1024,1,128]{3,1,2,0:T(8,128)(2,1)}, u32[]{:S(2)}, u32[]{:S(2)}) async-start(bf16[32,1024,1,128]{3,1,2,0:T(8,128)(2,1)} %fusion.43), calls=%async_computation | async-start | bytes 16777216 | tf_op jit(solution)/shard_map/all_to_all | solution.py:15
  136.6 3.6 copy-start.4
  136.6 3.6 copy-start.5
  174.6 8.2 %copy-start.2 = (bf16[9,1024,1024]{2,1,0:T(8,128)(2,1)S(1)}, bf16[9,1024,1024]{2,1,0:T(8,128)(2,1)}, u32[]{:S(2)}) copy-start(bf16[9,1024,1024]{2,1,0:T(8,128)(2,1)} %copy.65) | copy-start | bytes 56623108
  197.5 2.4 copy-start.6
  244.1 131.2 %all-to-all-start.1 = ((bf16[1024,32,128]{2,0,1:T(8,128)(2,1)}), bf16[1024,32,128]{2,0,1:T(8,128)(2,1)}, u32[]{:S(2)}, u32[]{:S(2)}) async-start(bf16[1024,32,128]{2,0,1:T(8,128)(2,1)} %scatter_fusion.1), calls=%async_computation.1 | async-start | bytes 16777216 | tf_op jit(solution)/shard_map/all_to_all | solution.py:149
  266.8 193.2 %all-gather.2.cloned.1.call-start = ((), (), s32[]{:S(2)}) async-start(), calls=%async_computation.3 | async-start | bytes 8650752 | tf_op jit(solution)/shard_map/all_gather | solution.py:111
  271.5 113.4 %copy-start.7 = (f32[1,31]{1,0:T(1,128)S(1)}, f32[1,31]{1,0:T(1,128)}, u32[]{:S(2)}) copy-start(f32[1,31]{1,0:T(1,128)} %param.15) | copy-start | bytes 376
  384.5 23.6 %copy-start.3 = (bf16[1024,128]{1,0:T(8,128)(2,1)S(1)}, bf16[1024,128]{1,0:T(8,128)(2,1)}, u32[]{:S(2)}) copy-start(bf16[1024,128]{1,0:T(8,128)(2,1)} %divide_convert_fusion) | copy-start | bytes 786436
  386.6 21.5 %collective-permute-start.1 = (bf16[1024,15]{1,0:T(8,128)(2,1)S(1)}, bf16[1024,15]{1,0:T(8,128)(2,1)S(1)}, u32[]{:S(2)}, u32[]{:S(2)}) collective-permute-start(bf16[1024,15]{1,0:T(8,128)(2,1)S(1)} %get-tuple-element.9), channel_id=1, source_target_pairs={{4,0},{8,4},{12,8},{16,12},{20,16},{24,20},{28,24},{32,28},{36,32}... | collective-permute-start | bytes 92168 | tf_op jit(solution)/shard_map/ppermute | solution.py:34
  392.2 15.9 %collective-permute-start = (bf16[1024,15]{1,0:T(8,128)(2,1)S(1)}, bf16[1024,15]{1,0:T(8,128)(2,1)S(1)}, u32[]{:S(2)}, u32[]{:S(2)}) collective-permute-start(bf16[1024,15]{1,0:T(8,128)(2,1)S(1)} %get-tuple-element.8), channel_id=1, source_target_pairs={{0,4},{4,8},{8,12},{12,16},{16,20},{20,24},{24,28},{28,32},{32,36}... | collective-permute-start | bytes 92168 | tf_op jit(solution)/shard_map/ppermute | solution.py:31
  409.8 11.0 %all-to-all-start.2 = ((f32[4,256,128]{2,1,0:T(8,128)}), f32[4,256,128]{2,1,0:T(8,128)S(1)}, u32[]{:S(2)}, u32[]{:S(2)}) async-start(f32[4,256,128]{2,1,0:T(8,128)} %bitcast.158), calls=%async_computation.2 | async-start | bytes 1048576 | tf_op jit(solution)/shard_map/all_to_all | solution.py:47
  489.3 10.9 %copy-start.1 = (s32[32,4,8]{0,2,1:T(8,128)S(1)}, s32[32,4,8]{0,2,1:T(8,128)}, u32[]{:S(2)}) copy-start(s32[32,4,8]{0,2,1:T(8,128)} %param.11) | copy-start | bytes 12292
Sparse Core Ops, SparseCore 0:
  384.7 75.1 all-gather.1
